TPU v7x, 512 devices: a whole 4x8x8 slice. The times are simulated.
512 devices in a mesh: dp: 2 (over core), tensor: 4 (over x), expert: 64 (over y, z).
Axes of the slice: x: 4, y: 8, z: 8, core: 2. Of those that a mesh axis runs over, the one named last changes fastest.
Arguments:
- checkpoint: bfloat16 [16384, 2048], P(('dp', 'expert'), 'tensor'), may hold values from -6 to 6
- scales: float32 [16384], P(('dp', 'expert')), may hold values from 0.5 to 2
- out_grad: bfloat16 [16384, 2048], P(('dp', 'expert'), 'tensor'), may hold values from -1.5 to 1.5
- expert_ids: int32 [16384, 8], P(('dp', 'expert')), may hold values from 0 to 127, all different within a row; in each aligned block of 128 rows (0 to 127, 128 to 255, ...) at most 8 rows name the same one
- gates: float32 [16384, 8], P(('dp', 'expert')), may hold values from 0.05 to 1
- w_gate: bfloat16 [128, 768, 2048], P(('dp', 'expert'), 'tensor'), may hold values from -0.125 to 0.125
- w_up: bfloat16 [128, 768, 2048], P(('dp', 'expert'), 'tensor'), may hold values from -0.125 to 0.125
- w_down: bfloat16 [128, 768, 2048], P(('dp', 'expert'), 'tensor'), may hold values from -0.21875 to 0.21875
Outputs:
- grad_input: bfloat16 [16384, 2048], P(('dp', 'expert'), 'tensor')
- grad_gates: float32 [16384, 8], P(('dp', 'expert'))
Inputs may be any that keep to these rules, and one draw needn't show every extreme that they name: `expert_ids`: each row names 8 different experts. Among the 128 rows of one device (aligned blocks of rows), no expert is named more than 8 times, a bound that some block reaches.
All inputs are finite; a program needn't handle non-finite values.
Results may differ from a plain program's by a relative error of at most 0.012.
Values may be sent and summed in bfloat16 or wider, within the bound.
A program may use at most 64 MiB of HBM per device.

v0:
```python
import jax
import jax.numpy as jnp
from jax import lax
from jax.sharding import PartitionSpec as P


def body(checkpoint, scales, out_grad, expert_ids, gates, w_gate, w_up, w_down):
    f32, bf16 = (jnp.float32, jnp.bfloat16)
    planes = lax.axis_size("tensor")
    experts = lax.axis_size("dp") * lax.axis_size("expert")
    rank = lax.axis_index("tensor")
    tokens, part = checkpoint.shape
    picks = expert_ids.shape[1]
    cap = tokens * picks // experts
    own = cap // planes
    width = part * planes
    wg = lax.all_gather(w_gate[0], "tensor", axis=0, tiled=True)
    wu = lax.all_gather(w_up[0], "tensor", axis=0, tiled=True)
    wd = lax.all_gather(w_down[0], "tensor", axis=0, tiled=True)
    dequant = (checkpoint.astype(f32) * scales[:, None]).astype(bf16)
    both = lax.all_gather(jnp.stack([dequant, out_grad]), "tensor", axis=2, tiled=True)
    named = expert_ids[:, :, None] == jnp.arange(experts, dtype=jnp.int32)[None, None, :]
    member = jnp.any(named, axis=1)
    weight = jnp.sum(jnp.where(named, gates[:, :, None], 0.0), axis=1)
    lower = (jnp.arange(tokens)[:, None] > jnp.arange(tokens)[None, :]).astype(bf16)
    place = jnp.dot(lower, member.astype(bf16), preferred_element_type=f32).astype(jnp.int32)
    slots = rank * own + jnp.arange(own, dtype=jnp.int32)
    pick = member.T[:, None, :] & (place.T[:, None, :] == slots[None, :, None])
    pick_rows = pick.reshape(experts * own, tokens)
    one = pick_rows.astype(bf16)
    send_x = jnp.dot(one, both[0], preferred_element_type=f32).astype(bf16)
    send_g = jnp.dot(one, both[1], preferred_element_type=f32).astype(bf16)
    names = ("dp", "expert")
    rows = lax.all_to_all(send_x.reshape(experts, own, width), names, 0, 0, tiled=True)
    grads = lax.all_to_all(send_g.reshape(experts, own, width), names, 0, 0, tiled=True)
    rows = rows.reshape(experts * own, width)
    grads = grads.reshape(experts * own, width)
    contract = (((1,), (1,)), ((), ()))
    gate_pre = lax.dot_general(rows, wg, contract, preferred_element_type=f32)
    up_pre = lax.dot_general(rows, wu, contract, preferred_element_type=f32)
    back = lax.dot_general(grads, wd, contract, preferred_element_type=f32)
    sigma = jax.nn.sigmoid(gate_pre)
    swish = gate_pre * sigma
    hidden = (swish * up_pre).astype(bf16)
    gate_term = jnp.sum(hidden.astype(f32) * back, axis=1)
    d_gate = (back * up_pre * sigma * (1.0 + gate_pre * (1.0 - sigma))).astype(bf16)
    d_up = (back * swish).astype(bf16)
    result = jnp.dot(d_gate, wg, preferred_element_type=f32)
    result = result + jnp.dot(d_up, wu, preferred_element_type=f32)
    tail = jnp.broadcast_to(gate_term[:, None], (experts * own, 128))
    packed = jnp.concatenate([result.astype(bf16), tail.astype(bf16)], axis=1)
    came = lax.all_to_all(packed.reshape(experts, own, width + 128), names, 0, 0, tiled=True)
    came = came.reshape(experts * own, width + 128)
    combine = jnp.where(pick, weight.T[:, None, :], 0.0).reshape(experts * own, tokens)
    high = combine.astype(bf16)
    low = (combine - high.astype(f32)).astype(bf16)
    flip = (((0,), (0,)), ((), ()))
    mixed = lax.dot_general(high, came[:, :width], flip, preferred_element_type=f32)
    mixed = mixed + lax.dot_general(low, came[:, :width], flip, preferred_element_type=f32)
    term = jnp.sum(
        jnp.where(pick, came[:, width].astype(f32).reshape(experts, own)[:, :, None], 0.0), axis=1
    )
    terms = jnp.sum(jnp.where(named, term.T[:, None, :], 0.0), axis=2)
    terms = jnp.pad(terms, ((0, 0), (0, 128 - picks))).astype(bf16)
    joined = jnp.concatenate(
        [
            mixed.astype(bf16).reshape(tokens, planes, part),
            jnp.broadcast_to(terms[:, None], (tokens, planes, 128)),
        ],
        axis=2,
    ).transpose(1, 0, 2)
    summed = lax.psum_scatter(joined, "tensor", scatter_dimension=0, tiled=True)[0]
    return (summed[:, :part], summed[:, part : part + picks].astype(f32))


def solution(mesh):
    return jax.shard_map(
        body,
        mesh=mesh,
        in_specs=(
            P(("dp", "expert"), "tensor"),
            P(("dp", "expert")),
            P(("dp", "expert"), "tensor"),
            P(("dp", "expert"), None),
            P(("dp", "expert"), None),
            P(("dp", "expert"), "tensor", None),
            P(("dp", "expert"), "tensor", None),
            P(("dp", "expert"), "tensor", None),
        ),
        out_specs=(P(("dp", "expert"), "tensor"), P(("dp", "expert"), None)),
        check_vma=False,
    )
```

profile of v0, /device:TPU:8, one launch (start us, length us, event | category | flops | bytes accessed | tf_op | source)
XLA Modules:
  0.0 274.9 jit_solution(13853421694187391772)
XLA Ops:
  7.2 0.0 all-gather.8.cloned.1.call-start
  7.2 1.0 fusion.24
  8.2 1.6 pad_maximum_fusion.1
  9.8 0.0 all-gather.8.cloned.1.call-update
  9.9 0.0 all-gather.14.cloned.1.call-start
  9.9 0.7 all-gather.14.cloned.1.call-update
  10.6 0.0 all-gather.12.cloned.1.call-start
  10.7 0.7 all-gather.12.cloned.1.call-update
  11.4 0.1 copy.29
  11.5 0.3 fusion.21
  11.7 0.1 copy.30
  11.9 0.2 convolution_convert_fusion.2
  12.1 0.2 compare_and_fusion
  12.2 0.1 and.32
  12.3 31.8 %all-gather.8.cloned.1.call-done = bf16[2,128,2048]{2,1,0:T(8,128)(2,1)} async-done(((bf16[2,128,512]{2,1,0:T(8,128)(2,1)}), bf16[2,128,2048]{2,1,0:T(8,128)(2,1)}) %all-gather.8.cloned.1.call-update) | async-done | bytes 1048592 | tf_op jit(solution)/shard_map/all_gather | solution.py:21
  44.1 1.5 convolution_convert_fusion
  45.6 1.5 reshape.113
  47.1 14.2 %all-to-all-start.1 = ((bf16[128,2,2048]{2,1,0:T(2,128)(2,1)}), bf16[128,2,2048]{2,1,0:T(2,128)(2,1)S(1)}, u32[]{:S(2)}, u32[]{:S(2)}) async-start(bf16[128,2,2048]{2,1,0:T(2,128)(2,1)} %reshape.113), calls=%async_computation.1 | async-start | bytes 2097152 | tf_op jit(solution)/shard_map/all_to_all | solution.py:34
  61.2 0.0 all-gather.10.cloned.1.call-start
  61.3 0.5 all-gather.10.cloned.1.call-update
  61.8 0.4 convolution_convert_fusion.1
  62.3 1.5 reshape.111
  63.8 28.5 %all-to-all-done.1 = bf16[128,2,2048]{2,1,0:T(2,128)(2,1)S(1)} async-done(((bf16[128,2,2048]{2,1,0:T(2,128)(2,1)}), bf16[128,2,2048]{2,1,0:T(2,128)(2,1)S(1)}, u32[]{:S(2)}, u32[]{:S(2)}) %all-to-all-start.1) | async-done | bytes 1048608 | tf_op jit(solution)/shard_map/all_to_all | solution.py:34
  92.2 7.5 %all-to-all-start = ((bf16[128,2,2048]{2,1,0:T(2,128)(2,1)}), bf16[128,2,2048]{2,1,0:T(2,128)(2,1)S(1)}, u32[]{:S(2)}, u32[]{:S(2)}) async-start(bf16[128,2,2048]{2,1,0:T(2,128)(2,1)} %reshape.111), calls=%async_computation | async-start | bytes 2097152 | tf_op jit(solution)/shard_map/all_to_all | solution.py:35
  99.7 0.4 reshape.114
  100.2 30.6 %all-to-all-done = bf16[128,2,2048]{2,1,0:T(2,128)(2,1)S(1)} async-done(((bf16[128,2,2048]{2,1,0:T(2,128)(2,1)}), bf16[128,2,2048]{2,1,0:T(2,128)(2,1)S(1)}, u32[]{:S(2)}, u32[]{:S(2)}) %all-to-all-start) | async-done | bytes 1048608 | tf_op jit(solution)/shard_map/all_to_all | solution.py:35
  130.7 0.4 reshape.112
  131.2 0.0 all-gather.14.cloned.1.call-done
  131.2 3.0 %fusion.2 = f32[256,768]{1,0:T(8,128)S(1)} fusion(bf16[256,2048]{1,0:T(8,128)(2,1)S(1)} %reshape.114, bf16[1,768,2048]{2,1,0:T(8,128)(2,1)} %all-gather.14.cloned.1.call-done), kind=kOutput, calls=%fused_computation.2 | convolution fusion | flops 805306368 | bytes 4980736 | tf_op jit(solution)/shard_map/dot_general | solution.py:39
  134.3 4.4 %all-gather.12.cloned.1.call-done = bf16[1,768,2048]{2,1,0:T(8,128)(2,1)} async-done(((bf16[1,192,2048]{2,1,0:T(8,128)(2,1)}), bf16[1,768,2048]{2,1,0:T(8,128)(2,1)}) %all-gather.12.cloned.1.call-update) | async-done | bytes 3145744 | tf_op jit(solution)/shard_map/all_gather | solution.py:18
  138.6 3.9 %fusion.6 = f32[256,768]{1,0:T(8,128)} fusion(bf16[256,2048]{1,0:T(8,128)(2,1)S(1)} %reshape.114, bf16[1,768,2048]{2,1,0:T(8,128)(2,1)} %all-gather.12.cloned.1.call-done), kind=kOutput, calls=%fused_computation.6 | convolution fusion | flops 805306368 | bytes 4980736 | tf_op jit(solution)/shard_map/dot_general | solution.py:40
  142.5 43.1 %all-gather.10.cloned.1.call-done = bf16[1,768,2048]{2,1,0:T(8,128)(2,1)} async-done(((bf16[1,192,2048]{2,1,0:T(8,128)(2,1)}), bf16[1,768,2048]{2,1,0:T(8,128)(2,1)}) %all-gather.10.cloned.1.call-update) | async-done | bytes 3145744 | tf_op jit(solution)/shard_map/all_gather | solution.py:19
  185.7 3.4 %multiply_reduce_fusion = (bf16[256]{0:T(256)(128)(2,1)S(1)}, f32[256,768]{1,0:T(8,128)S(1)}) fusion(f32[256,768]{1,0:T(8,128)} %fusion.6, f32[256,768]{1,0:T(8,128)S(1)} %fusion.2, bf16[256,2048]{1,0:T(8,128)(2,1)S(1)} %reshape.112, bf16[1,768,2048]{2,1,0:T(8,128)(2,1)} %all-gather.10.cloned.1.call-done), kind=kOutput, calls=%fused_computation.21 | convolution fusion | flops 807075584 | bytes 6554112 | tf_op jit(solution)/shard_map/dot_general | solution.py:41
  189.1 1.2 fusion
  190.3 0.7 copy-done.4
  191.0 1.1 fusion.13
  192.1 0.1 broadcast_in_dim.76
  192.2 0.1 pad_maximum_fusion
  192.3 0.0 copy-start.2
  192.3 1.3 reshape.115
  193.5 14.3 %all-to-all-start.2 = ((bf16[128,2,2176]{2,1,0:T(2,128)(2,1)}), bf16[128,2,2176]{2,1,0:T(2,128)(2,1)S(1)}, u32[]{:S(2)}, u32[]{:S(2)}) async-start(bf16[128,2,2176]{2,1,0:T(2,128)(2,1)} %reshape.115), calls=%async_computation.2 | async-start | bytes 2228224 | tf_op jit(solution)/shard_map/all_to_all | solution.py:52
  207.9 0.0 reduce-scatter.2.cloned.1.call-start
  208.0 0.1 copy.31
  208.1 0.1 and.28
  208.1 0.1 and.29
  208.2 0.1 eq.55
  208.4 32.1 %all-to-all-done.2 = bf16[128,2,2176]{2,1,0:T(2,128)(2,1)S(1)} async-done(((bf16[128,2,2176]{2,1,0:T(2,128)(2,1)}), bf16[128,2,2176]{2,1,0:T(2,128)(2,1)S(1)}, u32[]{:S(2)}, u32[]{:S(2)}) %all-to-all-start.2) | async-done | bytes 1114144 | tf_op jit(solution)/shard_map/all_to_all | solution.py:52
  240.4 0.4 reshape.116
  240.9 0.1 convert_reduce_fusion
  241.0 0.1 reshape.118
  241.2 0.3 select_reduce_fusion.2
  241.5 0.1 copy.33
  241.6 0.5 select_reduce_fusion.1
  242.1 0.1 copy.32
  242.3 0.4 fusion.18
  242.7 0.4 fusion.16
  243.2 0.3 copy.37
  243.4 0.1 copy.38
  243.6 0.9 maximum_bitcast_fusion
  244.4 0.0 reduce-scatter.2.cloned.1.call-update
  244.5 21.0 %reduce-scatter.2.cloned.1.call-done = bf16[1,128,640]{1,2,0:T(8,128)(2,1)} async-done(((bf16[4,128,640]{1,2,0:T(8,128)(2,1)}), bf16[1,128,640]{1,2,0:T(8,128)(2,1)}) %reduce-scatter.2.cloned.1.call-update) | async-done | bytes 163856 | tf_op jit(solution)/shard_map/reduce_scatter | solution.py:72
  265.5 0.9 slice.29
  266.4 1.3 slice_convert_fusion
  267.6 0.8 copy.36
  (16 shorter events, 0.2 us)
Async XLA Ops:
  7.2 4.2 %copy-start.1 = (s32[128,8]{0,1:T(8,128)S(1)}, s32[128,8]{0,1:T(8,128)}, u32[]{:S(2)}) copy-start(s32[128,8]{0,1:T(8,128)} %param.11) | copy-start | bytes 12292
  7.2 36.9 %all-gather.8.cloned.1.call-start = ((), (), s32[]{:S(2)}) async-start(), calls=%async_computation.4 | async-start | bytes 1310720 | tf_op jit(solution)/shard_map/all_gather | solution.py:21
  9.9 121.3 %all-gather.14.cloned.1.call-start = ((), (), s32[]{:S(2)}) async-start(), calls=%async_computation.8 | async-start | bytes 3932160 | tf_op jit(solution)/shard_map/all_gather | solution.py:17
  10.6 128.0 %all-gather.12.cloned.1.call-start = ((), (), s32[]{:S(2)}) async-start(), calls=%async_computation.7 | async-start | bytes 3932160 | tf_op jit(solution)/shard_map/all_gather | solution.py:18
  45.6 16.2 %copy-start = (bf16[2,128,2048]{2,1,0:T(8,128)(2,1)S(1)}, bf16[2,128,2048]{2,1,0:T(8,128)(2,1)}, u32[]{:S(2)}) copy-start(bf16[2,128,2048]{2,1,0:T(8,128)(2,1)} %all-gather.8.cloned.1.call-done) | copy-start | bytes 3145732
  47.1 45.2 %all-to-all-start.1 = ((bf16[128,2,2048]{2,1,0:T(2,128)(2,1)}), bf16[128,2,2048]{2,1,0:T(2,128)(2,1)S(1)}, u32[]{:S(2)}, u32[]{:S(2)}) async-start(bf16[128,2,2048]{2,1,0:T(2,128)(2,1)} %reshape.113), calls=%async_computation.1 | async-start | bytes 2097152 | tf_op jit(solution)/shard_map/all_to_all | solution.py:34
  61.2 124.4 %all-gather.10.cloned.1.call-start = ((), (), s32[]{:S(2)}) async-start(), calls=%async_computation.6 | async-start | bytes 3932160 | tf_op jit(solution)/shard_map/all_gather | solution.py:19
  92.2 38.5 %all-to-all-start = ((bf16[128,2,2048]{2,1,0:T(2,128)(2,1)}), bf16[128,2,2048]{2,1,0:T(2,128)(2,1)S(1)}, u32[]{:S(2)}, u32[]{:S(2)}) async-start(bf16[128,2,2048]{2,1,0:T(2,128)(2,1)} %reshape.111), calls=%async_computation | async-start | bytes 2097152 | tf_op jit(solution)/shard_map/all_to_all | solution.py:35
  185.7 3.4 %copy-start.3 = (bf16[1,768,2048]{2,1,0:T(8,128)(2,1)S(1)}, bf16[1,768,2048]{2,1,0:T(8,128)(2,1)}, u32[]{:S(2)}) copy-start(bf16[1,768,2048]{2,1,0:T(8,128)(2,1)} %all-gather.14.cloned.1.call-done) | copy-start | bytes 9437188
  185.7 3.4 %copy-start.5 = (f32[256,768]{1,0:T(8,128)S(1)}, f32[256,768]{1,0:T(8,128)}, u32[]{:S(2)}) copy-start(f32[256,768]{1,0:T(8,128)} %fusion.6) | copy-start | bytes 2359300
  189.1 1.9 copy-start.4
  192.3 15.7 %copy-start.2 = (f32[128,8]{0,1:T(8,128)S(1)}, f32[128,8]{0,1:T(8,128)}, u32[]{:S(2)}) copy-start(f32[128,8]{0,1:T(8,128)} %param.12) | copy-start | bytes 12292
  193.5 46.9 %all-to-all-start.2 = ((bf16[128,2,2176]{2,1,0:T(2,128)(2,1)}), bf16[128,2,2176]{2,1,0:T(2,128)(2,1)S(1)}, u32[]{:S(2)}, u32[]{:S(2)}) async-start(bf16[128,2,2176]{2,1,0:T(2,128)(2,1)} %reshape.115), calls=%async_computation.2 | async-start | bytes 2228224 | tf_op jit(solution)/shard_map/all_to_all | solution.py:52
  207.9 57.6 %reduce-scatter.2.cloned.1.call-start = ((), (), s32[]{:S(2)}) async-start(), calls=%async_computation.5 | async-start | bytes 819200 | tf_op jit(solution)/shard_map/reduce_scatter | solution.py:72
Sparse Core Ops, SparseCore 0:
  10.1 33.9 all-gather.7
  46.2 45.2 all-gather.13
  93.6 45.0 all-gather.11
  140.6 45.0 all-gather.9
  244.6 20.8 reduce-scatter.1
where the time goes:
time: 276 us; the launch traced here: 275 us
  waiting for transfers between devices  193 us (70%)
  starting transfers between devices  36.2 us (13%)
  matrix products  15.5 us (6%)
  between operations  14.1 us (5%)
  local copies, waits for them, and re-layouts  9.56 us (3%)
  other arithmetic  6.24 us (2%)
    all_gather x1, waiting for transfers between devices, body(): wd = lax.all_gather(w_down[0], 'tensor', axis=0, tiled=True)  43.1 us
    all_to_all x1, waiting for transfers between devices, body(): lax.all_to_all(packed.reshape(experts, own, width + 128), names, 0, 0, ti...  32.1 us
    all_gather x1, waiting for transfers between devices, body(): lax.all_gather(jnp.stack([dequant, out_grad]), 'tensor', axis=2, tiled=True)  31.8 us
    all_to_all x1, waiting for transfers between devices, body(): lax.all_to_all(send_g.reshape(experts, own, width), names, 0, 0, tiled=True)  30.6 us
    all_to_all x1, waiting for transfers between devices, body(): lax.all_to_all(send_x.reshape(experts, own, width), names, 0, 0, tiled=True)  28.5 us
    reduce_scatter x1, waiting for transfers between devices, body(): lax.psum_scatter(joined, 'tensor', scatter_dimension=0, tiled=True)[0]  21 us
    all_to_all x1, starting transfers between devices, body(): lax.all_to_all(packed.reshape(experts, own, width + 128), names, 0, 0, ti...  14.3 us
    all_to_all x1, starting transfers between devices, body(): lax.all_to_all(send_x.reshape(experts, own, width), names, 0, 0, tiled=True)  14.2 us
  transfers between devices with their start and end apart: 8, of which 7 were waited for; matrix products, arithmetic and copies ran while one was open for 5% of the time, Pallas kernels for 0%

commit v1 on v0

--- a/solution.py
+++ b/solution.py
@@ -16,7 +16,9 @@
     width = part * planes
     wg = lax.all_gather(w_gate[0], "tensor", axis=0, tiled=True)
     wu = lax.all_gather(w_up[0], "tensor", axis=0, tiled=True)
-    wd = lax.all_gather(w_down[0], "tensor", axis=0, tiled=True)
+    wd = jnp.concatenate(
+        lax.all_to_all(jnp.stack([w_down[0]] * lax.axis_size("tensor")), "tensor", 0, 0), axis=0
+    )
     dequant = (checkpoint.astype(f32) * scales[:, None]).astype(bf16)
     both = lax.all_gather(jnp.stack([dequant, out_grad]), "tensor", axis=2, tiled=True)
     named = expert_ids[:, :, None] == jnp.arange(experts, dtype=jnp.int32)[None, None, :]

time: 276 us -> 263 us (0.953)
  waiting for transfers between devices: 193 us -> 145 us
  blocking collectives: 0 us -> 38.4 us
  starting transfers between devices: 36.2 us -> 30.2 us
    all_gather x1 -> x0, waiting for transfers between devices: 43.1 us -> none  [body(): wd = lax.all_gather(w_down[0], 'tensor', axis=0, tiled=True)]
    all_to_all x0 -> x1, blocking collectives: none -> 38.4 us  [body(): lax.all_to_all(send_g.reshape(experts, own, width), names, 0, 0, tiled=True)]
    all_gather x1, waiting for transfers between devices: 4.39 us -> 0.02 us  [body(): wu = lax.all_gather(w_up[0], 'tensor', axis=0, tiled=True)]
    all_to_all x1, starting transfers between devices: 14.3 us -> 11.1 us  [body(): lax.all_to_all(packed.reshape(experts, own, width + 128), names, 0, 0, ti...]
  transfers between devices with their start and end apart: 8 -> 7, of which waited for: 7 -> 5; matrix products, arithmetic and copies ran while one was open for 5% -> 6% of each run, Pallas kernels for 0% -> 0%
where the time goes in v1:
time: 263 us; the launch traced here: 262 us
  waiting for transfers between devices  145 us (55%)
  blocking collectives  38.4 us (15%)
  starting transfers between devices  30.2 us (11%)
  matrix products  16.6 us (6%)
  between operations  14.1 us (5%)
  local copies, waits for them, and re-layouts  11.6 us (4%)
  other arithmetic  6.23 us (2%)
    all_to_all x1, blocking collectives, body(): lax.all_to_all(send_g.reshape(experts, own, width), names, 0, 0, tiled=True)  38.4 us
    all_to_all x1, waiting for transfers between devices, body(): lax.all_to_all(packed.reshape(experts, own, width + 128), names, 0, 0, ti...  32.1 us
    all_gather x1, waiting for transfers between devices, body(): lax.all_gather(jnp.stack([dequant, out_grad]), 'tensor', axis=2, tiled=True)  31.8 us
    all_to_all x1, waiting for transfers between devices, body(): lax.all_to_all(jnp.stack([w_down[0]] * lax.axis_size('tensor')), 'tensor'...  29.9 us
    all_to_all x1, waiting for transfers between devices, body(): lax.all_to_all(send_x.reshape(experts, own, width), names, 0, 0, tiled=True)  29.1 us
    reduce_scatter x1, waiting for transfers between devices, body(): lax.psum_scatter(joined, 'tensor', scatter_dimension=0, tiled=True)[0]  20.7 us
    all_to_all x1, starting transfers between devices, body(): lax.all_to_all(send_x.reshape(experts, own, width), names, 0, 0, tiled=True)  14.2 us
    all_to_all x1, starting transfers between devices, body(): lax.all_to_all(packed.reshape(experts, own, width + 128), names, 0, 0, ti...  11.1 us
  transfers between devices with their start and end apart: 7, of which 5 were waited for; matrix products, arithmetic and copies ran while one was open for 6% of the time, Pallas kernels for 0%

profile of v1, /device:TPU:8, one launch (start us, length us, event | category | flops | bytes accessed | tf_op | source)
XLA Modules:
  0.0 262.2 jit_solution(8399379794772489551)
XLA Ops:
  7.2 0.0 all-gather.6.cloned.1.call-start
  7.2 1.0 fusion.22
  8.2 1.6 pad_maximum_fusion.1
  9.8 0.0 all-gather.6.cloned.1.call-update
  9.9 0.0 all-gather.10.cloned.1.call-start
  9.9 0.7 all-gather.10.cloned.1.call-update
  10.6 0.8 copy.29
  11.4 0.3 fusion.19
  11.7 0.1 copy.30
  11.8 0.2 convolution_convert_fusion.2
  12.0 0.2 compare_and_fusion
  12.2 0.1 and.32
  12.3 31.8 %all-gather.6.cloned.1.call-done = bf16[2,128,2048]{2,1,0:T(8,128)(2,1)} async-done(((bf16[2,128,512]{2,1,0:T(8,128)(2,1)}), bf16[2,128,2048]{2,1,0:T(8,128)(2,1)}) %all-gather.6.cloned.1.call-update) | async-done | bytes 1048592 | tf_op jit(solution)/shard_map/all_gather | solution.py:23
  44.1 1.5 convolution_convert_fusion
  45.6 0.0 copy-start
  45.6 1.5 reshape.118
  47.1 14.2 %all-to-all-start.2 = ((bf16[128,2,2048]{2,1,0:T(2,128)(2,1)}), bf16[128,2,2048]{2,1,0:T(2,128)(2,1)S(1)}, u32[]{:S(2)}, u32[]{:S(2)}) async-start(bf16[128,2,2048]{2,1,0:T(2,128)(2,1)} %reshape.118), calls=%async_computation.2 | async-start | bytes 2097152 | tf_op jit(solution)/shard_map/all_to_all | solution.py:36
  61.3 0.0 all-gather.8.cloned.1.call-start
  61.3 0.7 all-gather.8.cloned.1.call-update
  62.0 0.4 convolution_convert_fusion.1
  62.5 0.7 reshape.115
  63.2 29.1 %all-to-all-done.2 = bf16[128,2,2048]{2,1,0:T(2,128)(2,1)S(1)} async-done(((bf16[128,2,2048]{2,1,0:T(2,128)(2,1)}), bf16[128,2,2048]{2,1,0:T(2,128)(2,1)S(1)}, u32[]{:S(2)}, u32[]{:S(2)}) %all-to-all-start.2) | async-done | bytes 1048608 | tf_op jit(solution)/shard_map/all_to_all | solution.py:36
  92.3 38.4 %all_to_all.20 = bf16[128,2,2048]{2,1,0:T(2,128)(2,1)S(1)} all-to-all(bf16[128,2,2048]{2,1,0:T(2,128)(2,1)S(1)} %reshape.115), channel_id=1, replica_groups=mesh['dp'=2,'tensor'=4,'expert'=64] {'dp','expert'}, dimensions={0} | all-to-all | bytes 2097152 | tf_op jit(solution)/shard_map/all_to_all | solution.py:37
  130.7 2.0 stack.15
  132.8 4.8 %all-to-all-start.1 = ((bf16[4,192,2048]{2,1,0:T(8,128)(2,1)}), bf16[4,192,2048]{2,1,0:T(8,128)(2,1)}, u32[]{:S(2)}, u32[]{:S(2)}) async-start(bf16[4,192,2048]{2,1,0:T(8,128)(2,1)} %stack.15), calls=%async_computation.1 | async-start | bytes 6291456 | tf_op jit(solution)/shard_map/all_to_all | solution.py:20
  137.6 0.4 reshape.119
  138.0 0.4 reshape.116
  138.5 0.0 all-gather.10.cloned.1.call-done
  138.5 2.9 %fusion.2 = f32[256,768]{1,0:T(8,128)S(1)} fusion(bf16[256,2048]{1,0:T(8,128)(2,1)S(1)} %reshape.119, bf16[1,768,2048]{2,1,0:T(8,128)(2,1)} %all-gather.10.cloned.1.call-done), kind=kOutput, calls=%fused_computation.2 | convolution fusion | flops 805306368 | bytes 4980736 | tf_op jit(solution)/shard_map/dot_general | solution.py:41
  141.4 0.0 all-gather.8.cloned.1.call-done
  141.5 4.1 %fusion.6 = f32[256,768]{1,0:T(8,128)} fusion(bf16[256,2048]{1,0:T(8,128)(2,1)S(1)} %reshape.119, bf16[1,768,2048]{2,1,0:T(8,128)(2,1)} %all-gather.8.cloned.1.call-done), kind=kOutput, calls=%fused_computation.6 | convolution fusion | flops 805306368 | bytes 4980736 | tf_op jit(solution)/shard_map/dot_general | solution.py:42
  145.5 29.9 %all-to-all-done.1 = bf16[4,192,2048]{2,1,0:T(8,128)(2,1)} async-done(((bf16[4,192,2048]{2,1,0:T(8,128)(2,1)}), bf16[4,192,2048]{2,1,0:T(8,128)(2,1)}, u32[]{:S(2)}, u32[]{:S(2)}) %all-to-all-start.1) | async-done | bytes 3145760 | tf_op jit(solution)/shard_map/all_to_all | solution.py:20
  175.5 3.4 %multiply_reduce_fusion = (bf16[256]{0:T(256)(128)(2,1)S(1)}, f32[256,768]{1,0:T(8,128)S(1)}) fusion(f32[256,768]{1,0:T(8,128)} %fusion.6, f32[256,768]{1,0:T(8,128)S(1)} %fusion.2, bf16[256,2048]{1,0:T(8,128)(2,1)S(1)} %reshape.116, bf16[768,2048]{1,0:T(8,128)(2,1)} %bitcast.8), kind=kOutput, calls=%fused_computation.19 | convolution fusion | flops 807075584 | bytes 6554112 | tf_op jit(solution)/shard_map/dot_general | solution.py:43
  178.9 1.1 fusion
  180.0 0.7 copy-done.4
  180.8 2.2 fusion.11
  183.0 0.1 broadcast_in_dim.76
  183.1 0.1 pad_maximum_fusion
  183.2 0.0 copy-start.2
  183.2 1.3 reshape.120
  184.4 11.1 %all-to-all-start.3 = ((bf16[128,2,2176]{2,1,0:T(2,128)(2,1)}), bf16[128,2,2176]{2,1,0:T(2,128)(2,1)S(1)}, u32[]{:S(2)}, u32[]{:S(2)}) async-start(bf16[128,2,2176]{2,1,0:T(2,128)(2,1)} %reshape.120), calls=%async_computation.3 | async-start | bytes 2228224 | tf_op jit(solution)/shard_map/all_to_all | solution.py:54
  195.5 0.0 reduce-scatter.2.cloned.1.call-start
  195.6 0.1 copy.31
  195.7 0.1 and.28
  195.7 0.1 and.29
  195.8 0.1 eq.55
  196.0 32.1 %all-to-all-done.3 = bf16[128,2,2176]{2,1,0:T(2,128)(2,1)S(1)} async-done(((bf16[128,2,2176]{2,1,0:T(2,128)(2,1)}), bf16[128,2,2176]{2,1,0:T(2,128)(2,1)S(1)}, u32[]{:S(2)}, u32[]{:S(2)}) %all-to-all-start.3) | async-done | bytes 1114144 | tf_op jit(solution)/shard_map/all_to_all | solution.py:54
  228.1 0.4 reshape.121
  228.5 0.1 convert_reduce_fusion
  228.6 0.1 reshape.123
  228.8 0.3 select_reduce_fusion.2
  229.1 0.1 copy.33
  229.2 0.5 select_reduce_fusion.1
  229.7 0.1 copy.32
  229.9 0.4 fusion.16
  230.3 0.4 fusion.14
  230.8 0.3 copy.37
  231.0 0.1 copy.38
  231.2 0.9 maximum_bitcast_fusion
  232.0 0.0 reduce-scatter.2.cloned.1.call-update
  232.1 20.7 %reduce-scatter.2.cloned.1.call-done = bf16[1,128,640]{1,2,0:T(8,128)(2,1)} async-done(((bf16[4,128,640]{1,2,0:T(8,128)(2,1)}), bf16[1,128,640]{1,2,0:T(8,128)(2,1)}) %reduce-scatter.2.cloned.1.call-update) | async-done | bytes 163856 | tf_op jit(solution)/shard_map/reduce_scatter | solution.py:74
  252.8 0.9 slice.29
  253.7 1.3 slice_convert_fusion
  254.9 0.8 copy.36
  (17 shorter events, 0.2 us)
Async XLA Ops:
  7.2 36.9 %all-gather.6.cloned.1.call-start = ((), (), s32[]{:S(2)}) async-start(), calls=%async_computation.5 | async-start | bytes 1310720 | tf_op jit(solution)/shard_map/all_gather | solution.py:23
  9.9 128.6 %all-gather.10.cloned.1.call-start = ((), (), s32[]{:S(2)}) async-start(), calls=%async_computation.8 | async-start | bytes 3932160 | tf_op jit(solution)/shard_map/all_gather | solution.py:17
  45.6 16.5 %copy-start = (bf16[2,128,2048]{2,1,0:T(8,128)(2,1)S(1)}, bf16[2,128,2048]{2,1,0:T(8,128)(2,1)}, u32[]{:S(2)}) copy-start(bf16[2,128,2048]{2,1,0:T(8,128)(2,1)} %all-gather.6.cloned.1.call-done) | copy-start | bytes 3145732
  47.1 45.2 %all-to-all-start.2 = ((bf16[128,2,2048]{2,1,0:T(2,128)(2,1)}), bf16[128,2,2048]{2,1,0:T(2,128)(2,1)S(1)}, u32[]{:S(2)}, u32[]{:S(2)}) async-start(bf16[128,2,2048]{2,1,0:T(2,128)(2,1)} %reshape.118), calls=%async_computation.2 | async-start | bytes 2097152 | tf_op jit(solution)/shard_map/all_to_all | solution.py:36
  61.3 80.2 %all-gather.8.cloned.1.call-start = ((), (), s32[]{:S(2)}) async-start(), calls=%async_computation.7 | async-start | bytes 3932160 | tf_op jit(solution)/shard_map/all_gather | solution.py:18
  92.3 38.4 %copy-start.1 = (bf16[1,192,2048]{2,1,0:T(8,128)(2,1)S(1)}, bf16[1,192,2048]{2,1,0:T(8,128)(2,1)}, u32[]{:S(2)}) copy-start(bf16[1,192,2048]{2,1,0:T(8,128)(2,1)} %param.15) | copy-start | bytes 2359300
  132.8 42.7 %all-to-all-start.1 = ((bf16[4,192,2048]{2,1,0:T(8,128)(2,1)}), bf16[4,192,2048]{2,1,0:T(8,128)(2,1)}, u32[]{:S(2)}, u32[]{:S(2)}) async-start(bf16[4,192,2048]{2,1,0:T(8,128)(2,1)} %stack.15), calls=%async_computation.1 | async-start | bytes 6291456 | tf_op jit(solution)/shard_map/all_to_all | solution.py:20
  141.4 37.4 %copy-start.5 = (f32[256,768]{1,0:T(8,128)}, f32[256,768]{1,0:T(8,128)S(1)}, u32[]{:S(2)}) copy-start(f32[256,768]{1,0:T(8,128)S(1)} %fusion.2) | copy-start | bytes 2359300
  175.5 3.4 %copy-start.3 = (bf16[1,768,2048]{2,1,0:T(8,128)(2,1)S(1)}, bf16[1,768,2048]{2,1,0:T(8,128)(2,1)}, u32[]{:S(2)}) copy-start(bf16[1,768,2048]{2,1,0:T(8,128)(2,1)} %all-gather.10.cloned.1.call-done) | copy-start | bytes 9437188
  175.5 3.4 %copy-start.6 = (f32[256,768]{1,0:T(8,128)S(1)}, f32[256,768]{1,0:T(8,128)}, u32[]{:S(2)}) copy-start(f32[256,768]{1,0:T(8,128)} %fusion.6) | copy-start | bytes 2359300
  178.9 1.9 copy-start.4
  183.2 12.4 %copy-start.2 = (f32[128,8]{0,1:T(8,128)S(1)}, f32[128,8]{0,1:T(8,128)}, u32[]{:S(2)}) copy-start(f32[128,8]{0,1:T(8,128)} %param.12) | copy-start | bytes 12292
  184.4 43.6 %all-to-all-start.3 = ((bf16[128,2,2176]{2,1,0:T(2,128)(2,1)}), bf16[128,2,2176]{2,1,0:T(2,128)(2,1)S(1)}, u32[]{:S(2)}, u32[]{:S(2)}) async-start(bf16[128,2,2176]{2,1,0:T(2,128)(2,1)} %reshape.120), calls=%async_computation.3 | async-start | bytes 2228224 | tf_op jit(solution)/shard_map/all_to_all | solution.py:54
  195.5 57.3 %reduce-scatter.2.cloned.1.call-start = ((), (), s32[]{:S(2)}) async-start(), calls=%async_computation.6 | async-start | bytes 819200 | tf_op jit(solution)/shard_map/reduce_scatter | solution.py:74
Sparse Core Ops, SparseCore 0:
  10.1 33.9 all-gather.5
  46.2 45.2 all-gather.9
  93.5 45.0 all-gather.7
  232.2 20.5 reduce-scatter.1
